TPU v7x, 32 devices: a whole 2x2x4 slice. The times are simulated.
32 devices in a mesh: dp: 8 (over z, y), grp: 4 (over x, core).
Axes of the slice: x: 2, y: 2, z: 4, core: 2. Of those that a mesh axis runs over, the one named last changes fastest.
Arguments:
- activations: bfloat16 [32, 512, 768], P('dp', None, 'grp'), may hold values from -6 to 6, as said below
- cotangent: bfloat16 [32, 512, 768], P('dp', None, 'grp'), may hold values from -6 to 6
- lengths: int32 [32], P('dp'), may hold values from 64 to 512
- triple_weight: bfloat16 [2, 4, 192, 576], P(None, 'grp'), may hold values from -0.25980762 to 0.25980762, as said below
- triple_bias: float32 [2, 2, 768], P(None, None, 'grp'), may hold values from -1.8 to 1.8, as said below
- output_weight: bfloat16 [2, 768, 768], replicated, may hold values from -1.75 to 1.75
- output_bias: float32 [2, 768], replicated, may hold values from -1.75 to 1.75
- first_gain: float32 [2, 768], replicated, may hold values from 0.25 to 1.75
- first_shift: float32 [2, 768], replicated, may hold values from -1.75 to 1.75
- widen_weight: bfloat16 [2, 4, 192, 768], P(None, 'grp'), may hold values from -0.4375 to 0.4375
- widen_bias: float32 [2, 3072], P(None, 'grp'), may hold values from -1.75 to 1.75
- shrink_weight: bfloat16 [2, 4, 768, 192], P(None, 'grp'), may hold values from -0.21875 to 0.21875
- narrow_bias: float32 [2, 768], P(None, 'grp'), may hold values from -1.75 to 1.75
- second_gain: float32 [2, 768], P(None, 'grp'), may hold values from 0.25 to 1.75
- second_shift: float32 [2, 768], P(None, 'grp'), may hold values from -1.75 to 1.75
Outputs:
- layer_output: bfloat16 [32, 512, 768], P('dp', None, 'grp')
- input_gradient: float32 [32, 512, 768], P('dp', None, 'grp')
- triple_weight_gradient: float32 [2, 4, 192, 576], P(None, 'grp')
- triple_bias_gradient: float32 [2, 2, 768], P(None, None, 'grp')
- output_weight_gradient: float32 [2, 768, 768], replicated
- output_bias_gradient: float32 [2, 768], replicated
- first_gain_gradient: float32 [2, 768], replicated
- first_shift_gradient: float32 [2, 768], replicated
- widen_weight_gradient: float32 [2, 4, 192, 768], P(None, 'grp')
- widen_bias_gradient: float32 [2, 3072], P(None, 'grp')
- narrow_weight_gradient: float32 [2, 4, 768, 192], P(None, 'grp')
- narrow_bias_gradient: float32 [2, 768], P(None, 'grp')
- second_norm_gain_gradient: float32 [2, 768], P(None, 'grp')
- second_shift_gradient: float32 [2, 768], P(None, 'grp')
Inputs may be any that keep to these rules, and one draw needn't show every extreme that they name: `activations`: independent entries of order one. `triple_weight`: independent entries with deviation about 192 ** -0.5. `triple_bias`: independent entries with deviation about 0.3.
All inputs are finite; a program needn't handle non-finite values.
Results may differ from a plain program's by a relative error of at most 0.015.
Values may be sent and summed in bfloat16 or wider, within the bound.
A program may use at most 192 MiB of HBM per device.

v0:
```python
import math
import jax
import jax.numpy as jnp
from jax import lax
from jax.sharding import PartitionSpec as P

HEAD = 64
EPSILON = 1e-05
MASKED = -1e30


def contract_rows(left, right):
    return lax.dot_general(
        left, right, (((0,), (0,)), ((), ())), preferred_element_type=jnp.float32
    )


def contract_cols(left, weight):
    return lax.dot_general(
        left, weight, (((1,), (1,)), ((), ())), preferred_element_type=jnp.float32
    )


def split_heads(block):
    return block.reshape(block.shape[0], block.shape[1] // HEAD, HEAD)


def score_block(queries, keys, length):
    scores = jnp.einsum(
        "qhd,khd->hqk", split_heads(queries), split_heads(keys), preferred_element_type=jnp.float32
    ) * HEAD ** (-0.5)
    visible = jnp.arange(keys.shape[0]) < length
    return jnp.where(visible[None, None, :], scores, MASKED)


def attend_forward(queries, keys, values, lengths):

    def single(inputs):
        query_one, key_one, value_one, length = inputs
        scores = score_block(query_one, key_one, length)
        highest = jnp.max(scores, axis=-1, keepdims=True)
        expon = jnp.exp(scores - highest)
        totals = jnp.sum(expon, axis=-1, keepdims=True)
        weights = (expon / totals).astype(jnp.bfloat16)
        mixed = jnp.einsum(
            "hqk,khd->qhd", weights, split_heads(value_one), preferred_element_type=jnp.float32
        )
        return (mixed.reshape(query_one.shape).astype(jnp.bfloat16), highest, totals)

    return lax.map(single, (queries, keys, values, lengths))


def attend_backward(queries, keys, values, outgrad, highest, totals, lengths):

    def single(inputs):
        query_one, key_one, value_one, grad_one, top, total, length = inputs
        scores = score_block(query_one, key_one, length)
        probs = jnp.exp(scores - top) / total
        weights = probs.astype(jnp.bfloat16)
        grad_heads = split_heads(grad_one)
        grad_probs = jnp.einsum(
            "qhd,khd->hqk", grad_heads, split_heads(value_one), preferred_element_type=jnp.float32
        )
        inner = jnp.sum(probs * grad_probs, axis=-1, keepdims=True)
        grad_scores = (probs * (grad_probs - inner)).astype(jnp.bfloat16)
        factor = HEAD ** (-0.5)
        query_grad = (
            jnp.einsum(
                "hqk,khd->qhd",
                grad_scores,
                split_heads(key_one),
                preferred_element_type=jnp.float32,
            )
            * factor
        )
        key_grad = (
            jnp.einsum(
                "hqk,qhd->khd",
                grad_scores,
                split_heads(query_one),
                preferred_element_type=jnp.float32,
            )
            * factor
        )
        value_grad = jnp.einsum(
            "hqk,qhd->khd", weights, grad_heads, preferred_element_type=jnp.float32
        )
        shape = query_one.shape
        return (
            query_grad.reshape(shape).astype(jnp.bfloat16),
            key_grad.reshape(shape).astype(jnp.bfloat16),
            value_grad.reshape(shape).astype(jnp.bfloat16),
        )

    return lax.map(single, (queries, keys, values, outgrad, highest, totals, lengths))


def gelu_slope(values):
    return 0.5 * (1.0 + lax.erf(values / math.sqrt(2.0))) + values * jnp.exp(
        -0.5 * values * values
    ) / math.sqrt(2.0 * math.pi)


def layer_forward(inputs, lengths, params, layer_params):
    (
        triple_weight,
        triple_bias,
        output_weight,
        output_bias,
        first_gain,
        first_shift,
        widen_weight,
        widen_bias,
        shrink_weight,
        narrow_bias,
        second_gain,
        second_shift,
    ) = params
    group_width = inputs.shape[-1]
    rows = inputs.reshape(-1, group_width)
    projected = jnp.dot(rows, triple_weight[layer_params, 0], preferred_element_type=jnp.float32)
    queries = (
        (projected[:, :group_width] + triple_bias[layer_params, 0])
        .astype(jnp.bfloat16)
        .reshape(inputs.shape)
    )
    keys = projected[:, group_width : 2 * group_width].astype(jnp.bfloat16).reshape(inputs.shape)
    values = (
        (projected[:, 2 * group_width :] + triple_bias[layer_params, 1])
        .astype(jnp.bfloat16)
        .reshape(inputs.shape)
    )
    queries, keys, values, residual = (
        lax.all_to_all(queries, "grp", split_axis=0, concat_axis=2, tiled=True),
        lax.all_to_all(keys, "grp", split_axis=0, concat_axis=2, tiled=True),
        lax.all_to_all(values, "grp", split_axis=0, concat_axis=2, tiled=True),
        lax.all_to_all(inputs, "grp", split_axis=0, concat_axis=2, tiled=True),
    )
    local = queries.shape[0]
    mine = lax.dynamic_slice_in_dim(lengths, lax.axis_index("grp") * local, local)
    attended, highest, totals = attend_forward(queries, keys, values, mine)
    width = attended.shape[-1]
    flat = attended.reshape(-1, width)
    before = (
        residual.reshape(-1, width).astype(jnp.float32)
        + jnp.dot(flat, output_weight[layer_params], preferred_element_type=jnp.float32)
        + output_bias[layer_params]
    )
    center = before - jnp.mean(before, axis=-1, keepdims=True)
    first_inverse = lax.rsqrt(jnp.mean(center * center, axis=-1, keepdims=True) + EPSILON)
    first_normed = center * first_inverse
    hidden = (
        (first_normed * first_gain[layer_params] + first_shift[layer_params])
        .astype(jnp.bfloat16)
        .reshape(attended.shape)
    )
    hidden_group = lax.all_to_all(hidden, "grp", split_axis=2, concat_axis=0, tiled=True)
    group_rows = hidden_group.reshape(-1, group_width)
    widened = (
        jnp.dot(group_rows, widen_weight[layer_params, 0], preferred_element_type=jnp.float32)
        + widen_bias[layer_params]
    )
    gelu_output = jax.nn.gelu(widened, approximate=False).astype(jnp.bfloat16)
    after = (
        group_rows.astype(jnp.float32)
        + jnp.dot(gelu_output, shrink_weight[layer_params, 0], preferred_element_type=jnp.float32)
        + narrow_bias[layer_params]
    )
    row_sum = jnp.sum(after, axis=-1)
    row_square = jnp.sum(after * after, axis=-1)
    total_sum, total_square = lax.psum((row_sum, row_square), "grp")
    average = (total_sum / width)[:, None]
    variance = (total_square / width)[:, None] - average * average
    second_inverse = lax.rsqrt(variance + EPSILON)
    second_normed = (after - average) * second_inverse
    output = (second_normed * second_gain[layer_params] + second_shift[layer_params]).reshape(
        inputs.shape
    )
    kept = (
        inputs,
        queries,
        keys,
        values,
        mine,
        highest,
        totals,
        attended,
        first_normed,
        first_inverse,
        group_rows,
        widened,
        gelu_output,
        second_normed,
        second_inverse,
    )
    return (output, kept)


def layer_backward(outgrad, params, layer_params, kept):
    (
        triple_weight,
        triple_bias,
        output_weight,
        output_bias,
        first_gain,
        first_shift,
        widen_weight,
        widen_bias,
        shrink_weight,
        narrow_bias,
        second_gain,
        second_shift,
    ) = params
    (
        inputs,
        queries,
        keys,
        values,
        mine,
        highest,
        totals,
        attended,
        first_normed,
        first_inverse,
        group_rows,
        widened,
        gelu_output,
        second_normed,
        second_inverse,
    ) = kept
    group_width = inputs.shape[-1]
    width = attended.shape[-1]
    grad_rows = outgrad.reshape(-1, group_width)
    scaled = grad_rows * second_gain[layer_params]
    part_sum = jnp.sum(scaled, axis=-1)
    part_cross = jnp.sum(scaled * second_normed, axis=-1)
    total_sum, total_cross = lax.psum((part_sum, part_cross), "grp")
    grad_after = second_inverse * (
        scaled - (total_sum / width)[:, None] - second_normed * (total_cross / width)[:, None]
    )
    second_gain_grad = jnp.sum(grad_rows * second_normed, axis=0)
    second_shift_grad = jnp.sum(grad_rows, axis=0)
    narrow_rounded = grad_after.astype(jnp.bfloat16)
    narrow_weight_grad = contract_rows(gelu_output, narrow_rounded)
    narrow_bias_grad = jnp.sum(narrow_rounded.astype(jnp.float32), axis=0)
    gelu_output_gradient = contract_cols(narrow_rounded, shrink_weight[layer_params, 0])
    widened_grad = (gelu_output_gradient * gelu_slope(widened)).astype(jnp.bfloat16)
    widen_weight_grad = contract_rows(group_rows, widened_grad)
    widen_bias_grad = jnp.sum(widened_grad.astype(jnp.float32), axis=0)
    hidden_grad = (grad_after + contract_cols(widened_grad, widen_weight[layer_params, 0])).astype(
        jnp.bfloat16
    )
    hidden_seq = lax.all_to_all(
        hidden_grad.reshape(inputs.shape), "grp", split_axis=0, concat_axis=2, tiled=True
    )
    seq_rows = hidden_seq.reshape(-1, width).astype(jnp.float32)
    first_gain_grad = jnp.sum(seq_rows * first_normed, axis=0)
    first_shift_grad = jnp.sum(seq_rows, axis=0)
    scaled_first = seq_rows * first_gain[layer_params]
    grad_before = first_inverse * (
        scaled_first
        - jnp.mean(scaled_first, axis=-1, keepdims=True)
        - first_normed * jnp.mean(scaled_first * first_normed, axis=-1, keepdims=True)
    )
    before_rounded = grad_before.astype(jnp.bfloat16)
    flat = attended.reshape(-1, width)
    output_weight_grad = contract_rows(flat, before_rounded)
    output_bias_grad = jnp.sum(before_rounded.astype(jnp.float32), axis=0)
    attended_grad = (
        contract_cols(before_rounded, output_weight[layer_params])
        .astype(jnp.bfloat16)
        .reshape(attended.shape)
    )
    residual_grad = before_rounded.reshape(attended.shape)
    query_seq, key_seq, value_seq = attend_backward(
        queries, keys, values, attended_grad, highest, totals, mine
    )
    query_grad, key_grad, value_grad, input_part = (
        lax.all_to_all(query_seq, "grp", split_axis=2, concat_axis=0, tiled=True),
        lax.all_to_all(key_seq, "grp", split_axis=2, concat_axis=0, tiled=True),
        lax.all_to_all(value_seq, "grp", split_axis=2, concat_axis=0, tiled=True),
        lax.all_to_all(residual_grad, "grp", split_axis=2, concat_axis=0, tiled=True),
    )
    triple_grad = jnp.concatenate(
        [
            query_grad.reshape(-1, group_width),
            key_grad.reshape(-1, group_width),
            value_grad.reshape(-1, group_width),
        ],
        axis=-1,
    )
    triple_weight_grad = contract_rows(inputs.reshape(-1, group_width), triple_grad)
    triple_bias_grad = jnp.stack(
        [
            jnp.sum(query_grad.reshape(-1, group_width).astype(jnp.float32), axis=0),
            jnp.sum(value_grad.reshape(-1, group_width).astype(jnp.float32), axis=0),
        ]
    )
    input_grad = contract_cols(triple_grad, triple_weight[layer_params, 0]) + input_part.reshape(
        -1, group_width
    ).astype(jnp.float32)
    grads = (
        triple_weight_grad[None],
        triple_bias_grad,
        output_weight_grad,
        output_bias_grad,
        first_gain_grad,
        first_shift_grad,
        widen_weight_grad[None],
        widen_bias_grad,
        narrow_weight_grad[None],
        narrow_bias_grad,
        second_gain_grad,
        second_shift_grad,
    )
    return (input_grad.reshape(inputs.shape), grads)


def shards(
    activations,
    cotangent,
    lengths,
    triple_weight,
    triple_bias,
    output_weight,
    output_bias,
    first_gain,
    first_shift,
    widen_weight,
    widen_bias,
    shrink_weight,
    narrow_bias,
    second_gain,
    second_shift,
):
    params = (
        triple_weight,
        triple_bias,
        output_weight,
        output_bias,
        first_gain,
        first_shift,
        widen_weight,
        widen_bias,
        shrink_weight,
        narrow_bias,
        second_gain,
        second_shift,
    )
    depth = triple_weight.shape[0]
    current = activations
    stored = []
    kept_list = []
    final = None
    for layer_params in range(depth):
        stored.append(current)
        result, kept = layer_forward(current, lengths, params, layer_params)
        kept_list.append(kept)
        final = result
        current = result.astype(jnp.bfloat16)
    outgrad = cotangent.astype(jnp.float32)
    collected = [None] * depth
    for layer_params in reversed(range(depth)):
        replayed, kept = layer_forward(stored[layer_params], lengths, params, layer_params)
        outgrad, layer_param_gradients = layer_backward(outgrad, params, layer_params, kept)
        collected[layer_params] = layer_param_gradients
    stacked = [
        jnp.stack([collected[layer_params][member] for layer_params in range(depth)])
        for member in range(12)
    ]
    group_totals = lax.psum(
        (
            stacked[0],
            stacked[1],
            stacked[6],
            stacked[7],
            stacked[8],
            stacked[9],
            stacked[10],
            stacked[11],
        ),
        "dp",
    )
    shared_totals = lax.psum((stacked[2], stacked[3], stacked[4], stacked[5]), ("dp", "grp"))
    return (
        final.astype(jnp.bfloat16),
        outgrad,
        group_totals[0],
        group_totals[1],
        shared_totals[0],
        shared_totals[1],
        shared_totals[2],
        shared_totals[3],
        group_totals[2],
        group_totals[3],
        group_totals[4],
        group_totals[5],
        group_totals[6],
        group_totals[7],
    )


def solution(mesh):
    in_specs = (
        P("dp", None, "grp"),
        P("dp", None, "grp"),
        P("dp"),
        P(None, "grp", None, None),
        P(None, None, "grp"),
        P(),
        P(),
        P(),
        P(),
        P(None, "grp", None, None),
        P(None, "grp"),
        P(None, "grp", None, None),
        P(None, "grp"),
        P(None, "grp"),
        P(None, "grp"),
    )
    out_specs = (
        P("dp", None, "grp"),
        P("dp", None, "grp"),
        P(None, "grp", None, None),
        P(None, None, "grp"),
        P(),
        P(),
        P(),
        P(),
        P(None, "grp", None, None),
        P(None, "grp"),
        P(None, "grp", None, None),
        P(None, "grp"),
        P(None, "grp"),
        P(None, "grp"),
    )
    return jax.shard_map(shards, mesh=mesh, in_specs=in_specs, out_specs=out_specs, check_vma=False)
```

profile of v0, /device:TPU:0, one launch (start us, length us, event | category | flops | bytes accessed | tf_op | source)
XLA Modules:
  0.0 857.9 jit_solution(8457950099970390052)
XLA Ops:
  7.2 4.4 all-to-all-start
  17.0 6.2 all-to-all-done
  31.4 6.9 all-to-all-done.3
  38.3 4.2 all-to-all-start.2
  45.1 9.1 %all-to-all-done.2 = bf16[4,512,192]{1,2,0:T(8,128)(2,1)} async-done(((bf16[4,512,192]{1,2,0:T(8,128)(2,1)}), bf16[4,512,192]{1,2,0:T(8,128)(2,1)}, u32[]{:S(2)}, u32[]{:S(2)}) %all-to-all-start.2) | async-done | bytes 786464 | tf_op jit(solution)/shard_map/all_to_all | solution.py:134
  57.7 10.6 %fusion.129 = (f32[12,512]{1,0:T(8,128)S(1)}, f32[12,512,512]{1,2,0:T(8,128)}) fusion(pred[512]{0:T(512)(128)(4,1)S(1)} %iota_compare_fusion, bf16[512,12,64]{0,2,1:T(8,128)(2,1)} %bitcast.12, bf16[512,12,64]{0,2,1:T(8,128)(2,1)S(1)} %bitcast.431), kind=kOutput, calls=%fused_computation.281 | convolution fusion | flops 415236608 | bytes 14180864 | tf_op jit(solution)/shard_map/while/body/eval_jaxpr/sub | solution.py:42
  69.4 6.1 fusion.61
  80.0 5.4 reduce.28
  91.6 10.4 %all-to-all-done.4 = bf16[4,2,49152]{2,1,0:T(2,128)(2,1)S(1)} async-done(((bf16[4,2,49152]{2,1,0:T(2,128)(2,1)}), bf16[4,2,49152]{2,1,0:T(2,128)(2,1)S(1)}, u32[]{:S(2)}, u32[]{:S(2)}) %all-to-all-start.4) | async-done | bytes 786464 | tf_op jit(solution)/shard_map/all_to_all | solution.py:157
  103.8 15.9 %fusion.6 = (bf16[2048,768]{1,0:T(8,128)(2,1)S(1)}, f32[2048,768]{1,0:T(8,128)}) fusion(f32[768]{0:T(1024)S(1)} %get-tuple-element.241, bf16[2048,192]{0,1:T(8,128)(2,1)S(1)} %bitcast.493, bf16[2,1,192,768]{3,2,1,0:T(8,128)(2,1)S(1)} %copy-done.66), kind=kOutput, calls=%fused_computation.18 | convolution fusion | flops 707788800 | bytes 10522624 | tf_op jit(solution)/shard_map/dot_general | solution.py:160
  121.4 10.1 %all-reduce.6 = (f32[2048]{0:T(1024)S(1)}, f32[2048]{0:T(1024)S(1)}) all-reduce(f32[2048]{0:T(1024)S(1)} %get-tuple-element.233, f32[2048]{0:T(1024)S(1)} %get-tuple-element.232), channel_id=1, replica_groups=mesh['dp'=8,'grp'=4] {'grp'}, use_global_device_ids=true, to_apply=%region_7.8 | all-reduce | flops 4096 | bytes 32768 | tf_op jit(solution)/shard_map/psum | solution.py:171
  142.1 6.6 all-to-all-done.5
  148.7 3.7 all-to-all-start.8
  155.4 8.5 all-to-all-done.8
  164.0 4.2 all-to-all-start.7
  171.0 8.9 %all-to-all-done.7 = bf16[4,512,192]{1,2,0:T(8,128)(2,1)} async-done(((bf16[4,512,192]{1,2,0:T(8,128)(2,1)}), bf16[4,512,192]{1,2,0:T(8,128)(2,1)}, u32[]{:S(2)}, u32[]{:S(2)}) %all-to-all-start.7) | async-done | bytes 786464 | tf_op jit(solution)/shard_map/all_to_all | solution.py:134
  183.4 10.5 %fusion.131 = (f32[12,512]{1,0:T(8,128)S(1)}, f32[12,512,512]{1,2,0:T(8,128)}) fusion(pred[512]{0:T(512)(128)(4,1)S(1)} %iota_compare_fusion, bf16[512,12,64]{0,2,1:T(8,128)(2,1)} %bitcast.37, bf16[512,12,64]{0,2,1:T(8,128)(2,1)S(1)} %bitcast.433), kind=kOutput, calls=%fused_computation.283 | convolution fusion | flops 415236608 | bytes 14180864 | tf_op jit(solution)/shard_map/while/body/eval_jaxpr/sub | solution.py:42
  195.0 6.1 fusion.67
  203.7 3.9 copy.152
  207.6 6.3 reduce.29
  216.3 4.2 all-to-all-start.9
  221.9 10.4 %all-to-all-done.9 = bf16[4,2,49152]{2,1,0:T(2,128)(2,1)} async-done(((bf16[4,2,49152]{2,1,0:T(2,128)(2,1)}), bf16[4,2,49152]{2,1,0:T(2,128)(2,1)}, u32[]{:S(2)}, u32[]{:S(2)}) %all-to-all-start.9) | async-done | bytes 786464 | tf_op jit(solution)/shard_map/all_to_all | solution.py:157
  232.2 3.7 reshape.510
  238.5 15.8 %fusion.9 = (bf16[2048,768]{1,0:T(8,128)(2,1)S(1)}, f32[2048,768]{1,0:T(8,128)}) fusion(f32[768]{0:T(1024)S(1)} %get-tuple-element.240, bf16[2048,192]{0,1:T(8,128)(2,1)S(1)} %bitcast.497, bf16[2,1,192,768]{3,2,1,0:T(8,128)(2,1)S(1)} %copy-done.67), kind=kOutput, calls=%fused_computation.21 | convolution fusion | flops 707788800 | bytes 10522624 | tf_op jit(solution)/shard_map/dot_general | solution.py:160
  256.7 10.3 %all-reduce.5 = (f32[2048]{0:T(1024)S(1)}, f32[2048]{0:T(1024)S(1)}) all-reduce(f32[2048]{0:T(1024)S(1)} %get-tuple-element.231, f32[2048]{0:T(1024)S(1)} %get-tuple-element.230), channel_id=1, replica_groups=mesh['dp'=8,'grp'=4] {'grp'}, use_global_device_ids=true, to_apply=%region_15.16 | all-reduce | flops 4096 | bytes 32768 | tf_op jit(solution)/shard_map/psum | solution.py:171
  269.4 10.3 %all-reduce.4 = (f32[2048]{0:T(1024)S(1)}, f32[2048]{0:T(1024)S(1)}) all-reduce(f32[2048]{0:T(1024)S(1)} %get-tuple-element.223, f32[2048]{0:T(1024)S(1)} %bitcast.523), channel_id=1, replica_groups=mesh['dp'=8,'grp'=4] {'grp'}, use_global_device_ids=true, to_apply=%region_19.20 | all-reduce | flops 4096 | bytes 32768 | tf_op jit(solution)/shard_map/psum | solution.py:237
  279.7 4.1 convert_reduce_fusion.3
  283.9 6.3 convert_reduce_fusion
  292.8 4.2 all-to-all-start.10
  297.1 11.6 %all-to-all-done.10 = bf16[4,512,192]{1,2,0:T(8,128)(2,1)} async-done(((bf16[4,512,192]{1,2,0:T(8,128)(2,1)}), bf16[4,512,192]{1,2,0:T(8,128)(2,1)}, u32[]{:S(2)}, u32[]{:S(2)}) %all-to-all-start.10) | async-done | bytes 786464 | tf_op jit(solution)/shard_map/all_to_all | solution.py:253
  322.3 6.9 fusion.70
  330.5 6.3 reduce.33
  342.8 11.6 %multiply_reduce_fusion.1 = (f32[12,512]{1,0:T(8,128)S(1)}, f32[12,512,512]{1,2,0:T(8,128)}) fusion(f32[12,512,512]{1,2,0:T(8,128)} %get-tuple-element.302, f32[12,512]{1,0:T(8,128)S(1)} %get-tuple-element.301, bf16[512,12,64]{0,2,1:T(8,128)(2,1)} %bitcast.513, bf16[512,12,64]{0,2,1:T(8,128)(2,1)} %bitcast.510), kind=kOutput, calls=%fused_computation.5 | convolution fusion | flops 412084224 | bytes 26787840 | tf_op jit(solution)/shard_map/while/body/eval_jaxpr/qhd,khd->hqk/dot_general | solution.py:61
  357.3 6.4 reduce.30
  365.1 4.6 all-to-all-start.14
  369.7 9.6 %multiply_convert_fusion.1 = bf16[12,512,512]{1,2,0:T(8,128)(2,1)S(1)} fusion(f32[12,512,512]{1,2,0:T(8,128)} %get-tuple-element.309, f32[12,512]{1,0:T(8,128)S(1)} %get-tuple-element.308, f32[12,512,512]{1,2,0:T(8,128)} %get-tuple-element.302, f32[12,512]{1,0:T(8,128)S(1)} %get-tuple-element.301), kind=kLoop, calls=%fused_computation.4 | loop fusion | flops 12582912 | bytes 31506432 | tf_op jit(solution)/shard_map/while/body/eval_jaxpr/convert_element_type | solution.py:65
  379.3 3.7 multiply_convert_fusion.5
  385.4 6.5 reduce.32
  393.3 4.4 all-to-all-start.12
  397.7 3.9 multiply_convert_fusion.6
  404.0 6.4 reduce.31
  411.8 4.4 all-to-all-start.11
  440.9 11.9 %all-reduce.3 = (f32[2048]{0:T(1024)S(1)}, f32[2048]{0:T(1024)S(1)}) all-reduce(f32[2048]{0:T(1024)S(1)} %get-tuple-element.221, f32[2048]{0:T(1024)S(1)} %get-tuple-element.228), channel_id=1, replica_groups=mesh['dp'=8,'grp'=4] {'grp'}, use_global_device_ids=true, to_apply=%region_26.27 | all-reduce | flops 4096 | bytes 32768 | tf_op jit(solution)/shard_map/psum | solution.py:237
  454.8 6.3 convert_reduce_fusion.1
  463.8 4.6 all-to-all-start.15
  476.3 3.8 all-to-all-done.15
  489.2 6.7 fusion.64
  495.9 8.9 %multiply_reduce_fusion = (f32[12,512]{1,0:T(8,128)S(1)}, f32[12,512,512]{1,2,0:T(8,128)}) fusion(f32[12,512,512]{1,2,0:T(8,128)} %get-tuple-element.295, f32[12,512]{1,0:T(8,128)S(1)} %copy-done.81, bf16[512,12,64]{0,2,1:T(8,128)(2,1)S(1)} %bitcast.515, bf16[512,12,64]{0,2,1:T(8,128)(2,1)S(1)} %bitcast.508), kind=kOutput, calls=%fused_computation.3 | convolution fusion | flops 412084224 | bytes 26787840 | tf_op jit(solution)/shard_map/while/body/eval_jaxpr/qhd,khd->hqk/dot_general | solution.py:61
  506.0 5.4 reduce.37
  512.8 4.4 all-to-all-start.18
  517.2 9.6 %multiply_convert_fusion = bf16[12,512,512]{1,2,0:T(8,128)(2,1)S(1)} fusion(f32[12,512,512]{1,2,0:T(8,128)} %get-tuple-element.312, f32[12,512]{1,0:T(8,128)S(1)} %get-tuple-element.311, f32[12,512,512]{1,2,0:T(8,128)} %get-tuple-element.295, f32[12,512]{1,0:T(8,128)S(1)} %copy-done.81), kind=kLoop, calls=%fused_computation.2 | loop fusion | flops 12582912 | bytes 31506432 | tf_op jit(solution)/shard_map/while/body/eval_jaxpr/convert_element_type | solution.py:65
  526.8 3.7 multiply_convert_fusion.2
  531.8 5.4 reduce.36
  542.1 4.2 all-to-all-start.17
  546.5 4.2 pad_maximum_fusion
  551.8 3.9 multiply_convert_fusion.3
  558.1 7.5 reduce.35
  568.0 4.2 all-to-all-start.16
  601.3 6.3 reduce.34
  610.0 4.2 all-to-all-start.19
  614.4 47.1 %all-reduce = (f32[2,768]{1,0:T(2,128)}, f32[2,768]{1,0:T(2,128)}, f32[2,768]{1,0:T(2,128)}) all-reduce(f32[2,768]{1,0:T(2,128)S(1)} %pad_maximum_fusion.4, f32[2,768]{1,0:T(2,128)S(1)} %pad_maximum_fusion.5, f32[2,768]{1,0:T(2,128)S(1)} %pad_maximum_fusion.6), channel_id=1, replica_groups=mesh['dp'=8,'grp'=4] {'dp','grp'}, use_global_device_ids=true, to_apply=%region_39.40 | all-reduce | flops 4608 | bytes 36864 | tf_op jit(solution)/shard_map/psum | solution.py:384
  668.6 37.8 %all-reduce.1 = (f32[2,2,192]{2,1,0:T(2,128)}, f32[2,768]{1,0:T(2,128)}, f32[2,192]{1,0:T(2,128)}, f32[2,192]{1,0:T(2,128)}, f32[2,192]{1,0:T(2,128)}) all-reduce(f32[2,2,192]{2,1,0:T(2,128)S(1)} %pad_maximum_fusion.8, f32[2,768]{1,0:T(2,128)S(1)} %pad_maximum_fusion.7, ...), channel_id=1, replica_groups=mesh['dp'=8,'grp'=4] {'dp'}, use_global_device_ids=true, to_apply=%region_35.36 | all-reduce | flops 3456 | bytes 27648 | tf_op jit(solution)/shard_map/psum | solution.py:371
  706.3 134.4 %all-reduce.12.cloned.1.call-done = (f32[2,1,192,576]{3,2,1,0:T(8,128)}, f32[2,1,192,768]{3,2,1,0:T(8,128)}, f32[2,1,768,192]{2,3,1,0:T(8,128)}) async-done(((f32[2,1,192,576]{3,2,1,0:T(8,128)}, f32[2,1,192,768]{3,2,1,0:T(8,128)}, f32[2,1,768,192]{2,3,1,0:T(8,128)}), (f32[2,1,192,576]{3,2,1,0:T(8,128)}, f32[2,1,192,768]{3,2,1,0:T(8,128)}, f32[2,1,768,192]{2,3,1,0:T(8,128)})) %all-reduce.12.cloned.1.call-update) | async-done | bytes 3244048 | tf_op jit(solution)/shard_map/psum | solution.py:371
  843.0 4.9 copy.272
  (426 shorter events, 208.2 us)
Async XLA Ops:
  7.2 16.0 %all-to-all-start = ((bf16[4,512,192]{1,2,0:T(8,128)(2,1)}), bf16[4,512,192]{1,2,0:T(8,128)(2,1)S(1)}, u32[]{:S(2)}, u32[]{:S(2)}) async-start(bf16[4,512,192]{1,2,0:T(8,128)(2,1)} %param.15), calls=%async_computation | async-start | bytes 1572864 | tf_op jit(solution)/shard_map/all_to_all | solution.py:137
  15.9 10.8 %copy-start.96 = (f32[2,2,192]{2,1,0:T(2,128)S(1)}, f32[2,2,192]{2,1,0:T(2,128)}, u32[]{:S(2)}) copy-start(f32[2,2,192]{2,1,0:T(2,128)} %param.19) | copy-start | bytes 9220
  23.2 15.1 %all-to-all-start.3 = ((bf16[4,512,192]{1,2,0:T(8,128)(2,1)}), bf16[4,512,192]{1,2,0:T(8,128)(2,1)S(1)}, u32[]{:S(2)}, u32[]{:S(2)}) async-start(bf16[4,512,192]{1,2,0:T(8,128)(2,1)} %bitcast.407), calls=%async_computation.3 | async-start | bytes 1572864 | tf_op jit(solution)/shard_map/all_to_all | solution.py:135
  28.9 14.3 %copy-start.87 = (f32[2,768]{1,0:T(2,128)S(1)}, f32[2,768]{1,0:T(2,128)}, u32[]{:S(2)}) copy-start(f32[2,768]{1,0:T(2,128)} %param.21) | copy-start | bytes 18436
  28.9 14.3 %copy-start.88 = (f32[2,768]{1,0:T(2,128)S(1)}, f32[2,768]{1,0:T(2,128)}, u32[]{:S(2)}) copy-start(f32[2,768]{1,0:T(2,128)} %param.23) | copy-start | bytes 18436
  28.9 14.3 %copy-start.89 = (f32[2,768]{1,0:T(2,128)S(1)}, f32[2,768]{1,0:T(2,128)}, u32[]{:S(2)}) copy-start(f32[2,768]{1,0:T(2,128)} %param.22) | copy-start | bytes 18436
  38.3 19.4 %copy-start.32 = (bf16[4,512,192]{1,2,0:T(8,128)(2,1)}, bf16[4,512,192]{1,2,0:T(8,128)(2,1)S(1)}, u32[]{:S(2)}) copy-start(bf16[4,512,192]{1,2,0:T(8,128)(2,1)S(1)} %all-to-all-done.3) | copy-start | bytes 2359300
  38.3 15.9 %all-to-all-start.2 = ((bf16[4,512,192]{1,2,0:T(8,128)(2,1)}), bf16[4,512,192]{1,2,0:T(8,128)(2,1)}, u32[]{:S(2)}, u32[]{:S(2)}) async-start(bf16[4,512,192]{1,2,0:T(8,128)(2,1)} %bitcast.408), calls=%async_computation.2 | async-start | bytes 1572864 | tf_op jit(solution)/shard_map/all_to_all | solution.py:134
  43.3 33.6 %copy-start.74 = (f32[768]{0:T(1024)}, f32[768]{0:T(1024)S(1)}, u32[]{:S(2)}) copy-start(f32[768]{0:T(1024)S(1)} %get-tuple-element.317) | copy-start | bytes 9220
  54.2 15.1 %all-to-all-start.1 = ((bf16[4,512,192]{1,2,0:T(8,128)(2,1)}), bf16[4,512,192]{1,2,0:T(8,128)(2,1)S(1)}, u32[]{:S(2)}, u32[]{:S(2)}) async-start(bf16[4,512,192]{1,2,0:T(8,128)(2,1)} %bitcast.409), calls=%async_computation.1 | async-start | bytes 1572864 | tf_op jit(solution)/shard_map/all_to_all | solution.py:136
  68.4 7.1 copy-start.80
  76.8 8.6 %copy-start.78 = (f32[512]{0:T(512)}, f32[512]{0:T(512)S(1)}, u32[]{:S(2)}) copy-start(f32[512]{0:T(512)S(1)} %add_rsqrt_fusion.3) | copy-start | bytes 6148
  79.4 10.9 %copy-start.99 = (f32[2,192]{1,0:T(2,128)S(1)}, f32[2,192]{1,0:T(2,128)}, u32[]{:S(2)}) copy-start(f32[2,192]{1,0:T(2,128)} %param.27) | copy-start | bytes 4612
  79.5 11.5 %copy-start.90 = (f32[2,768]{1,0:T(2,128)S(1)}, f32[2,768]{1,0:T(2,128)}, u32[]{:S(2)}) copy-start(f32[2,768]{1,0:T(2,128)} %param.25) | copy-start | bytes 18436
  79.5 11.5 %copy-start.100 = (f32[2,192]{1,0:T(2,128)S(1)}, f32[2,192]{1,0:T(2,128)}, u32[]{:S(2)}) copy-start(f32[2,192]{1,0:T(2,128)} %param.28) | copy-start | bytes 4612
  79.5 11.5 %copy-start.101 = (f32[2,192]{1,0:T(2,128)S(1)}, f32[2,192]{1,0:T(2,128)}, u32[]{:S(2)}) copy-start(f32[2,192]{1,0:T(2,128)} %param.29) | copy-start | bytes 4612
  86.8 15.1 %all-to-all-start.4 = ((bf16[4,2,49152]{2,1,0:T(2,128)(2,1)}), bf16[4,2,49152]{2,1,0:T(2,128)(2,1)S(1)}, u32[]{:S(2)}, u32[]{:S(2)}) async-start(bf16[4,2,49152]{2,1,0:T(2,128)(2,1)} %reshape.507), calls=%async_computation.4 | async-start | bytes 1572864 | tf_op jit(solution)/shard_map/all_to_all | solution.py:157
  91.0 12.8 %copy-start.93 = (f32[768]{0:T(1024)}, f32[768]{0:T(1024)S(1)}, u32[]{:S(2)}) copy-start(f32[768]{0:T(1024)S(1)} %get-tuple-element.241) | copy-start | bytes 9220
  91.0 40.6 %copy-start.82 = (f32[1,192]{1,0:T(1,128)}, f32[1,192]{1,0:T(1,128)S(1)}, u32[]{:S(2)}) copy-start(f32[1,192]{1,0:T(1,128)S(1)} %get-tuple-element.289) | copy-start | bytes 2308
  103.7 15.9 %copy-start.47 = (bf16[24,8,4,512]{3,1,2,0:T(8,128)(2,1)}, bf16[24,8,4,512]{3,1,2,0:T(8,128)(2,1)S(1)}, u32[]{:S(2)}) copy-start(bf16[24,8,4,512]{3,1,2,0:T(8,128)(2,1)S(1)} %copy.218) | copy-start | bytes 2359300
  103.8 15.9 %copy-start.107 = (bf16[2,1,768,192]{2,3,1,0:T(8,128)(2,1)S(1)}, bf16[2,1,768,192]{2,3,1,0:T(8,128)(2,1)}, u32[]{:S(2)}) copy-start(bf16[2,1,768,192]{2,3,1,0:T(8,128)(2,1)} %param.26) | copy-start | bytes 1769476
  121.4 17.4 %copy-start.16 = (f32[2048,192]{0,1:T(8,128)}, f32[2048,192]{0,1:T(8,128)S(1)}, u32[]{:S(2)}) copy-start(f32[2048,192]{0,1:T(8,128)S(1)} %get-tuple-element.300) | copy-start | bytes 4718596
  133.5 15.1 %all-to-all-start.5 = ((bf16[4,512,192]{1,2,0:T(8,128)(2,1)}), bf16[4,512,192]{1,2,0:T(8,128)(2,1)S(1)}, u32[]{:S(2)}, u32[]{:S(2)}) async-start(bf16[4,512,192]{1,2,0:T(8,128)(2,1)} %bitcast.406), calls=%async_computation.5 | async-start | bytes 1572864 | tf_op jit(solution)/shard_map/all_to_all | solution.py:137
  148.7 15.3 %all-to-all-start.8 = ((bf16[4,512,192]{1,2,0:T(8,128)(2,1)}), bf16[4,512,192]{1,2,0:T(8,128)(2,1)S(1)}, u32[]{:S(2)}, u32[]{:S(2)}) async-start(bf16[4,512,192]{1,2,0:T(8,128)(2,1)} %bitcast.403), calls=%async_computation.8 | async-start | bytes 1572864 | tf_op jit(solution)/shard_map/all_to_all | solution.py:135
  164.0 19.4 %copy-start.34 = (bf16[4,512,192]{1,2,0:T(8,128)(2,1)}, bf16[4,512,192]{1,2,0:T(8,128)(2,1)S(1)}, u32[]{:S(2)}) copy-start(bf16[4,512,192]{1,2,0:T(8,128)(2,1)S(1)} %all-to-all-done.8) | copy-start | bytes 2359300
  164.0 15.9 %all-to-all-start.7 = ((bf16[4,512,192]{1,2,0:T(8,128)(2,1)}), bf16[4,512,192]{1,2,0:T(8,128)(2,1)}, u32[]{:S(2)}, u32[]{:S(2)}) async-start(bf16[4,512,192]{1,2,0:T(8,128)(2,1)} %bitcast.404), calls=%async_computation.7 | async-start | bytes 1572864 | tf_op jit(solution)/shard_map/all_to_all | solution.py:134
  179.9 15.1 %all-to-all-start.6 = ((bf16[4,512,192]{1,2,0:T(8,128)(2,1)}), bf16[4,512,192]{1,2,0:T(8,128)(2,1)S(1)}, u32[]{:S(2)}, u32[]{:S(2)}) async-start(bf16[4,512,192]{1,2,0:T(8,128)(2,1)} %bitcast.405), calls=%async_computation.6 | async-start | bytes 1572864 | tf_op jit(solution)/shard_map/all_to_all | solution.py:136
  213.9 6.6 copy-start.42
  216.3 15.9 %all-to-all-start.9 = ((bf16[4,2,49152]{2,1,0:T(2,128)(2,1)}), bf16[4,2,49152]{2,1,0:T(2,128)(2,1)}, u32[]{:S(2)}, u32[]{:S(2)}) async-start(bf16[4,2,49152]{2,1,0:T(2,128)(2,1)} %reshape.509), calls=%async_computation.9 | async-start | bytes 1572864 | tf_op jit(solution)/shard_map/all_to_all | solution.py:157
  221.9 45.1 %copy-start.14 = (f32[4,24,8,512]{3,2,0,1:T(8,128)}, f32[4,24,8,512]{3,2,0,1:T(8,128)S(1)}, u32[]{:S(2)}) copy-start(f32[4,24,8,512]{3,2,0,1:T(8,128)S(1)} %copy.217) | copy-start | bytes 4718596
  238.4 15.9 %copy-start.48 = (bf16[24,8,4,512]{3,1,2,0:T(8,128)(2,1)}, bf16[24,8,4,512]{3,1,2,0:T(8,128)(2,1)S(1)}, u32[]{:S(2)}) copy-start(bf16[24,8,4,512]{3,1,2,0:T(8,128)(2,1)S(1)} %copy.219) | copy-start | bytes 2359300
  238.5 15.9 %copy-start.102 = (f32[1,192]{1,0:T(1,128)S(1)}, f32[1,192]{1,0:T(1,128)}, u32[]{:S(2)}) copy-start(f32[1,192]{1,0:T(1,128)} %get-tuple-element.292) | copy-start | bytes 2308
  238.5 15.9 %copy-start.108 = (bf16[2,1,768,192]{2,3,1,0:T(8,128)(2,1)S(1)}, bf16[2,1,768,192]{2,3,1,0:T(8,128)(2,1)}, u32[]{:S(2)}) copy-start(bf16[2,1,768,192]{2,3,1,0:T(8,128)(2,1)} %param.26) | copy-start | bytes 1769476
  256.7 23.0 %copy-start.98 = (f32[1,192]{1,0:T(1,128)S(1)}, f32[1,192]{1,0:T(1,128)}, u32[]{:S(2)}) copy-start(f32[1,192]{1,0:T(1,128)} %get-tuple-element.290) | copy-start | bytes 2308
  283.9 6.3 copy-start.68
  292.8 15.9 %all-to-all-start.10 = ((bf16[4,512,192]{1,2,0:T(8,128)(2,1)}), bf16[4,512,192]{1,2,0:T(8,128)(2,1)}, u32[]{:S(2)}, u32[]{:S(2)}) async-start(bf16[4,512,192]{1,2,0:T(8,128)(2,1)} %bitcast.474), calls=%async_computation.10 | async-start | bytes 1572864 | tf_op jit(solution)/shard_map/all_to_all | solution.py:253
  322.3 6.9 copy-start.63
  339.1 26.0 %all-to-all-start.13 = ((bf16[4,2,49152]{2,1,0:T(2,128)(2,1)}), bf16[4,2,49152]{2,1,0:T(2,128)(2,1)S(1)}, u32[]{:S(2)}, u32[]{:S(2)}) async-start(bf16[4,2,49152]{2,1,0:T(2,128)(2,1)} %reshape.517), calls=%async_computation.13 | async-start | bytes 1572864 | tf_op jit(solution)/shard_map/all_to_all | solution.py:281
  342.8 11.6 %copy-start.26 = (bf16[512,768]{1,0:T(8,128)(2,1)S(1)}, bf16[512,768]{1,0:T(8,128)(2,1)}, u32[]{:S(2)}) copy-start(bf16[512,768]{1,0:T(8,128)(2,1)} %copy-done.25) | copy-start | bytes 2359300
  365.1 14.2 %copy-start.43 = (bf16[4,2,49152]{2,1,0:T(2,128)(2,1)}, bf16[4,2,49152]{2,1,0:T(2,128)(2,1)S(1)}, u32[]{:S(2)}) copy-start(bf16[4,2,49152]{2,1,0:T(2,128)(2,1)S(1)} %all-to-all-done.13) | copy-start | bytes 2359300
  365.1 28.2 %all-to-all-start.14 = ((bf16[4,2,49152]{2,1,0:T(2,128)(2,1)}), bf16[4,2,49152]{2,1,0:T(2,128)(2,1)}, u32[]{:S(2)}, u32[]{:S(2)}) async-start(bf16[4,2,49152]{2,1,0:T(2,128)(2,1)} %reshape.511), calls=%async_computation.14 | async-start | bytes 1572864 | tf_op jit(solution)/shard_map/all_to_all | solution.py:282
  385.4 12.2 %copy-start.75 = (f32[768]{0:T(1024)S(1)}, f32[768]{0:T(1024)}, u32[]{:S(2)}) copy-start(f32[768]{0:T(1024)} %copy-done.74) | copy-start | bytes 9220
  385.4 12.3 %copy-start.35 = (bf16[4,512,192]{1,2,0:T(8,128)(2,1)S(1)}, bf16[4,512,192]{1,2,0:T(8,128)(2,1)}, u32[]{:S(2)}) copy-start(bf16[4,512,192]{1,2,0:T(8,128)(2,1)} %copy-done.34) | copy-start | bytes 2359300
  393.3 18.5 %all-to-all-start.12 = ((bf16[4,2,49152]{2,1,0:T(2,128)(2,1)}), bf16[4,2,49152]{2,1,0:T(2,128)(2,1)}, u32[]{:S(2)}, u32[]{:S(2)}) async-start(bf16[4,2,49152]{2,1,0:T(2,128)(2,1)} %reshape.515), calls=%async_computation.12 | async-start | bytes 1572864 | tf_op jit(solution)/shard_map/all_to_all | solution.py:280
  411.8 22.0 %all-to-all-start.11 = ((bf16[4,2,49152]{2,1,0:T(2,128)(2,1)}), bf16[4,2,49152]{2,1,0:T(2,128)(2,1)}, u32[]{:S(2)}, u32[]{:S(2)}) async-start(bf16[4,2,49152]{2,1,0:T(2,128)(2,1)} %reshape.513), calls=%async_computation.11 | async-start | bytes 1572864 | tf_op jit(solution)/shard_map/all_to_all | solution.py:279
  440.9 13.9 %copy-start.94 = (f32[768]{0:T(1024)S(1)}, f32[768]{0:T(1024)}, u32[]{:S(2)}) copy-start(f32[768]{0:T(1024)} %copy-done.93) | copy-start | bytes 9220
  440.9 13.9 %copy-start.109 = (bf16[2,1,768,192]{2,3,1,0:T(8,128)(2,1)S(1)}, bf16[2,1,768,192]{2,3,1,0:T(8,128)(2,1)}, u32[]{:S(2)}) copy-start(bf16[2,1,768,192]{2,3,1,0:T(8,128)(2,1)} %param.26) | copy-start | bytes 1769476
  454.8 6.3 copy-start.10
  463.8 16.3 %all-to-all-start.15 = ((bf16[4,512,192]{1,2,0:T(8,128)(2,1)}), bf16[4,512,192]{1,2,0:T(8,128)(2,1)}, u32[]{:S(2)}, u32[]{:S(2)}) async-start(bf16[4,512,192]{1,2,0:T(8,128)(2,1)} %bitcast.473), calls=%async_computation.15 | async-start | bytes 1572864 | tf_op jit(solution)/shard_map/all_to_all | solution.py:253
  476.3 9.8 %copy-start.5 = (f32[512,768]{1,0:T(8,128)S(1)}, f32[512,768]{1,0:T(8,128)}, u32[]{:S(2)}) copy-start(f32[512,768]{1,0:T(8,128)} %copy-done.4) | copy-start | bytes 4718596
  476.3 9.8 %copy-start.77 = (f32[512]{0:T(512)S(1)}, f32[512]{0:T(512)}, u32[]{:S(2)}) copy-start(f32[512]{0:T(512)} %copy-done.76) | copy-start | bytes 6148
  476.3 9.8 %copy-start.79 = (f32[512]{0:T(512)S(1)}, f32[512]{0:T(512)}, u32[]{:S(2)}) copy-start(f32[512]{0:T(512)} %copy-done.78) | copy-start | bytes 6148
  489.2 6.7 copy-start.61
  512.8 29.3 %all-to-all-start.18 = ((bf16[4,2,49152]{2,1,0:T(2,128)(2,1)}), bf16[4,2,49152]{2,1,0:T(2,128)(2,1)}, u32[]{:S(2)}, u32[]{:S(2)}) async-start(bf16[4,2,49152]{2,1,0:T(2,128)(2,1)} %reshape.525), calls=%async_computation.18 | async-start | bytes 1572864 | tf_op jit(solution)/shard_map/all_to_all | solution.py:281
  530.6 8.0 copy-start.29
  538.6 8.0 copy-start.20
  542.1 25.9 %all-to-all-start.17 = ((bf16[4,2,49152]{2,1,0:T(2,128)(2,1)}), bf16[4,2,49152]{2,1,0:T(2,128)(2,1)}, u32[]{:S(2)}, u32[]{:S(2)}) async-start(bf16[4,2,49152]{2,1,0:T(2,128)(2,1)} %reshape.523), calls=%async_computation.17 | async-start | bytes 1572864 | tf_op jit(solution)/shard_map/all_to_all | solution.py:280
  546.3 160.1 %all-reduce.10.cloned.1.call-start = ((), (), s32[]{:S(2)}) async-start(), calls=%async_computation.20 | async-start | bytes 9437184 | tf_op jit(solution)/shard_map/psum | solution.py:384
  558.1 14.1 %copy-start.9 = (bf16[2048,768]{1,0:T(8,128)(2,1)S(1)}, bf16[2048,768]{1,0:T(8,128)(2,1)}, u32[]{:S(2)}) copy-start(bf16[2048,768]{1,0:T(8,128)(2,1)} %copy-done.8) | copy-start | bytes 9437188
  568.0 19.9 %all-to-all-start.16 = ((bf16[4,2,49152]{2,1,0:T(2,128)(2,1)}), bf16[4,2,49152]{2,1,0:T(2,128)(2,1)}, u32[]{:S(2)}, u32[]{:S(2)}) async-start(bf16[4,2,49152]{2,1,0:T(2,128)(2,1)} %reshape.521), calls=%async_computation.16 | async-start | bytes 1572864 | tf_op jit(solution)/shard_map/all_to_all | solution.py:279
  572.2 268.6 %all-reduce.12.cloned.1.call-start = ((), (), s32[]{:S(2)}) async-start(), calls=%async_computation.21 | async-start | bytes 6684672 | tf_op jit(solution)/shard_map/psum | solution.py:371
  601.3 12.9 %copy-start.91 = (f32[192]{0:T(256)S(1)}, f32[192]{0:T(256)}, u32[]{:S(2)}) copy-start(f32[192]{0:T(256)} %get-tuple-element.234) | copy-start | bytes 2308
  601.3 12.9 %copy-start.97 = (f32[192]{0:T(256)S(1)}, f32[192]{0:T(256)}, u32[]{:S(2)}) copy-start(f32[192]{0:T(256)} %get-tuple-element.273) | copy-start | bytes 2308
  610.0 51.5 %all-to-all-start.19 = ((bf16[4,2,49152]{2,1,0:T(2,128)(2,1)}), bf16[4,2,49152]{2,1,0:T(2,128)(2,1)}, u32[]{:S(2)}, u32[]{:S(2)}) async-start(bf16[4,2,49152]{2,1,0:T(2,128)(2,1)} %reshape.519), calls=%async_computation.19 | async-start | bytes 1572864 | tf_op jit(solution)/shard_map/all_to_all | solution.py:282
  (69 other events, 193.3 us)
Sparse Core Ops, SparseCore 0:
  553.3 147.5 all-reduce.9
  706.6 134.1 all-reduce.11
where the time goes:
time: 869 us; the launch traced here: 858 us
  waiting for transfers between devices  219 us (25%)
  matrix products  162 us (19%)
  local copies, waits for them, and re-layouts  131 us (15%)
  blocking collectives  127 us (15%)
  other arithmetic  121 us (14%)
  starting transfers between devices  81.2 us (9%)
  between operations  16.6 us (2%)
    psum x1, waiting for transfers between devices, shards(): lax.psum((stacked[0], stacked[1], stacked[6], stacked[7], stacked[8], sta...  134 us
    unnamed x270, local copies, waits for them, and re-layouts  76.3 us
    unnamed x11, other arithmetic  62.1 us
    psum x1, blocking collectives, shards(): lax.psum((stacked[2], stacked[3], stacked[4], stacked[5]), ('dp', 'grp'))  47.1 us
    psum x1, blocking collectives, shards(): lax.psum((stacked[0], stacked[1], stacked[6], stacked[7], stacked[8], sta...  37.8 us
    dot_general x2, matrix products, layer_forward(): jnp.dot(group_rows, widen_weight[layer_params, 0], preferred_element_type...  31.7 us
    psum x2, blocking collectives, layer_backward(): total_sum, total_cross = lax.psum((part_sum, part_cross), 'grp')  22.2 us
    sub x2, matrix products, single(): expon = jnp.exp(scores - highest)  21.1 us
  transfers between devices with their start and end apart: 22, of which 13 were waited for; matrix products, arithmetic and copies ran while one was open for 25% of the time, Pallas kernels for 0%

commit v1 on v0

--- a/solution.py
+++ b/solution.py
@@ -7,6 +7,29 @@
 HEAD = 64
 EPSILON = 1e-05
 MASKED = -1e30
+
+
+def cut_along(array, dim, length):
+    shape = array.shape
+    blocks = array.reshape(*shape[:dim], length, shape[dim] // length, *shape[dim + 1 :])
+    return jnp.moveaxis(blocks, dim, 0)
+
+
+def laid_out(parts, dim):
+    parts = jnp.moveaxis(parts, 0, dim)
+    dims = parts.shape
+    return parts.reshape(*dims[:dim], dims[dim] * dims[dim + 1], *dims[dim + 2 :])
+
+
+def exchange_in_pairs(shard, axis, split_dim, concat_dim):
+    count, index = (lax.axis_size(axis), lax.axis_index(axis))
+    parts = cut_along(shard, split_dim, count)
+    outs = [parts[index]]
+    for step in range(1, count):
+        sent = parts[index ^ step]
+        outs.append(lax.ppermute(sent, axis, [(i, i ^ step) for i in range(count)]))
+    parts = jnp.stack(outs)[index ^ jnp.arange(count)]
+    return laid_out(parts, concat_dim)
 
 
 def contract_rows(left, right):
@@ -250,9 +273,7 @@
     hidden_grad = (grad_after + contract_cols(widened_grad, widen_weight[layer_params, 0])).astype(
         jnp.bfloat16
     )
-    hidden_seq = lax.all_to_all(
-        hidden_grad.reshape(inputs.shape), "grp", split_axis=0, concat_axis=2, tiled=True
-    )
+    hidden_seq = exchange_in_pairs(hidden_grad.reshape(inputs.shape), "grp", 0, 2)
     seq_rows = hidden_seq.reshape(-1, width).astype(jnp.float32)
     first_gain_grad = jnp.sum(seq_rows * first_normed, axis=0)
     first_shift_grad = jnp.sum(seq_rows, axis=0)

time: 869 us -> 873 us (level)
  local copies, waits for them, and re-layouts: 131 us -> 146 us
    all_to_all x2 -> x0, waiting for transfers between devices: 15.4 us -> none  [layer_backward(): lax.all_to_all(hidden_grad.reshape(inputs.shape), 'grp', split_axis=0, co...]
    ppermute x0 -> x6, waiting for transfers between devices: none -> 11 us  [exchange_in_pairs(): outs.append(lax.ppermute(sent, axis, [(i, i ^ step) for i in range(count)]))]
    all_to_all x2 -> x0, starting transfers between devices: 8.78 us -> none  [layer_backward(): lax.all_to_all(hidden_grad.reshape(inputs.shape), 'grp', split_axis=0, co...]
    unnamed x270 -> x280, local copies, waits for them, and re-layouts: 76.3 us -> 81.2 us
  transfers between devices with their start and end apart: 22 -> 26, of which waited for: 13 -> 15; matrix products, arithmetic and copies ran while one was open for 25% -> 25% of each run, Pallas kernels for 0% -> 0%
where the time goes in v1:
time: 873 us; the launch traced here: 863 us
  waiting for transfers between devices  214 us (25%)
  matrix products  161 us (18%)
  local copies, waits for them, and re-layouts  146 us (17%)
  blocking collectives  128 us (15%)
  other arithmetic  121 us (14%)
  starting transfers between devices  76.8 us (9%)
  between operations  16.7 us (2%)
    psum x1, waiting for transfers between devices, shards(): lax.psum((stacked[0], stacked[1], stacked[6], stacked[7], stacked[8], sta...  134 us
    unnamed x280, local copies, waits for them, and re-layouts  81.2 us
    unnamed x11, other arithmetic  63.2 us
    psum x1, blocking collectives, shards(): lax.psum((stacked[2], stacked[3], stacked[4], stacked[5]), ('dp', 'grp'))  47.4 us
    psum x1, blocking collectives, shards(): lax.psum((stacked[0], stacked[1], stacked[6], stacked[7], stacked[8], sta...  37.8 us
    dot_general x2, matrix products, layer_forward(): jnp.dot(group_rows, widen_weight[layer_params, 0], preferred_element_type...  31.7 us
    psum x2, blocking collectives, layer_backward(): total_sum, total_cross = lax.psum((part_sum, part_cross), 'grp')  22.4 us
    sub x2, matrix products, single(): expon = jnp.exp(scores - highest)  21.1 us
  transfers between devices with their start and end apart: 26, of which 15 were waited for; matrix products, arithmetic and copies ran while one was open for 25% of the time, Pallas kernels for 0%

profile of v1, /device:TPU:0, one launch (start us, length us, event | category | flops | bytes accessed | tf_op | source)
XLA Modules:
  0.0 862.6 jit_solution(10795794559348769253)
XLA Ops:
  7.2 4.4 all-to-all-start
  17.0 6.2 all-to-all-done
  31.4 6.9 all-to-all-done.3
  38.3 4.2 all-to-all-start.2
  45.1 9.1 %all-to-all-done.2 = bf16[4,512,192]{1,2,0:T(8,128)(2,1)} async-done(((bf16[4,512,192]{1,2,0:T(8,128)(2,1)}), bf16[4,512,192]{1,2,0:T(8,128)(2,1)}, u32[]{:S(2)}, u32[]{:S(2)}) %all-to-all-start.2) | async-done | bytes 786464 | tf_op jit(solution)/shard_map/all_to_all | solution.py:157
  57.7 10.6 %fusion.130 = (f32[12,512]{1,0:T(8,128)S(1)}, f32[12,512,512]{1,2,0:T(8,128)}) fusion(pred[512]{0:T(512)(128)(4,1)S(1)} %iota_compare_fusion, bf16[512,12,64]{0,2,1:T(8,128)(2,1)} %bitcast.12, bf16[512,12,64]{0,2,1:T(8,128)(2,1)S(1)} %bitcast.469), kind=kOutput, calls=%fused_computation.300 | convolution fusion | flops 415236608 | bytes 14180864 | tf_op jit(solution)/shard_map/while/body/eval_jaxpr/sub | solution.py:65
  69.4 6.1 fusion.61
  80.0 5.4 reduce.28
  91.6 10.4 %all-to-all-done.4 = bf16[4,2,49152]{2,1,0:T(2,128)(2,1)S(1)} async-done(((bf16[4,2,49152]{2,1,0:T(2,128)(2,1)}), bf16[4,2,49152]{2,1,0:T(2,128)(2,1)S(1)}, u32[]{:S(2)}, u32[]{:S(2)}) %all-to-all-start.4) | async-done | bytes 786464 | tf_op jit(solution)/shard_map/all_to_all | solution.py:180
  103.8 15.9 %fusion.6 = (bf16[2048,768]{1,0:T(8,128)(2,1)S(1)}, f32[2048,768]{1,0:T(8,128)}) fusion(f32[768]{0:T(1024)S(1)} %get-tuple-element.241, bf16[2048,192]{0,1:T(8,128)(2,1)S(1)} %bitcast.527, bf16[2,1,192,768]{3,2,1,0:T(8,128)(2,1)S(1)} %copy-done.67), kind=kOutput, calls=%fused_computation.20 | convolution fusion | flops 707788800 | bytes 10522624 | tf_op jit(solution)/shard_map/dot_general | solution.py:183
  121.4 10.1 %all-reduce.6 = (f32[2048]{0:T(1024)S(1)}, f32[2048]{0:T(1024)S(1)}) all-reduce(f32[2048]{0:T(1024)S(1)} %get-tuple-element.233, f32[2048]{0:T(1024)S(1)} %get-tuple-element.232), channel_id=1, replica_groups=mesh['dp'=8,'grp'=4] {'grp'}, use_global_device_ids=true, to_apply=%region_7.8 | all-reduce | flops 4096 | bytes 32768 | tf_op jit(solution)/shard_map/psum | solution.py:194
  142.1 6.6 all-to-all-done.5
  148.6 3.7 all-to-all-start.8
  155.4 8.5 all-to-all-done.8
  164.0 4.2 all-to-all-start.7
  171.0 8.9 %all-to-all-done.7 = bf16[4,512,192]{1,2,0:T(8,128)(2,1)} async-done(((bf16[4,512,192]{1,2,0:T(8,128)(2,1)}), bf16[4,512,192]{1,2,0:T(8,128)(2,1)}, u32[]{:S(2)}, u32[]{:S(2)}) %all-to-all-start.7) | async-done | bytes 786464 | tf_op jit(solution)/shard_map/all_to_all | solution.py:157
  183.4 10.5 %fusion.132 = (f32[12,512]{1,0:T(8,128)S(1)}, f32[12,512,512]{1,2,0:T(8,128)}) fusion(pred[512]{0:T(512)(128)(4,1)S(1)} %iota_compare_fusion, bf16[512,12,64]{0,2,1:T(8,128)(2,1)} %bitcast.37, bf16[512,12,64]{0,2,1:T(8,128)(2,1)S(1)} %bitcast.471), kind=kOutput, calls=%fused_computation.302 | convolution fusion | flops 415236608 | bytes 14180864 | tf_op jit(solution)/shard_map/while/body/eval_jaxpr/sub | solution.py:65
  195.0 6.1 fusion.67
  203.7 3.9 copy.174
  207.6 6.3 reduce.29
  216.3 4.2 all-to-all-start.9
  222.6 9.6 %all-to-all-done.9 = bf16[4,2,49152]{2,1,0:T(2,128)(2,1)} async-done(((bf16[4,2,49152]{2,1,0:T(2,128)(2,1)}), bf16[4,2,49152]{2,1,0:T(2,128)(2,1)}, u32[]{:S(2)}, u32[]{:S(2)}) %all-to-all-start.9) | async-done | bytes 786464 | tf_op jit(solution)/shard_map/all_to_all | solution.py:180
  232.2 3.7 reshape.526
  238.5 15.9 %fusion.9 = (bf16[2048,768]{1,0:T(8,128)(2,1)S(1)}, f32[2048,768]{1,0:T(8,128)}) fusion(f32[768]{0:T(1024)S(1)} %get-tuple-element.240, bf16[2048,192]{0,1:T(8,128)(2,1)S(1)} %bitcast.531, bf16[2,1,192,768]{3,2,1,0:T(8,128)(2,1)S(1)} %copy-done.68), kind=kOutput, calls=%fused_computation.23 | convolution fusion | flops 707788800 | bytes 10522624 | tf_op jit(solution)/shard_map/dot_general | solution.py:183
  256.7 10.3 %all-reduce.5 = (f32[2048]{0:T(1024)S(1)}, f32[2048]{0:T(1024)S(1)}) all-reduce(f32[2048]{0:T(1024)S(1)} %get-tuple-element.231, f32[2048]{0:T(1024)S(1)} %get-tuple-element.230), channel_id=1, replica_groups=mesh['dp'=8,'grp'=4] {'grp'}, use_global_device_ids=true, to_apply=%region_15.16 | all-reduce | flops 4096 | bytes 32768 | tf_op jit(solution)/shard_map/psum | solution.py:194
  269.4 10.1 %all-reduce.4 = (f32[2048]{0:T(1024)S(1)}, f32[2048]{0:T(1024)S(1)}) all-reduce(f32[2048]{0:T(1024)S(1)} %get-tuple-element.223, f32[2048]{0:T(1024)S(1)} %bitcast.569), channel_id=1, replica_groups=mesh['dp'=8,'grp'=4] {'grp'}, use_global_device_ids=true, to_apply=%region_19.20 | all-reduce | flops 4096 | bytes 32768 | tf_op jit(solution)/shard_map/psum | solution.py:260
  279.6 4.1 convert_reduce_fusion.3
  283.7 6.3 convert_reduce_fusion
  296.9 3.8 constant_dynamic-slice_fusion.7
  303.1 5.3 collective-permute-done.1
  326.6 6.9 fusion.70
  334.7 6.5 reduce.33
  347.1 11.6 %multiply_reduce_fusion.1 = (f32[12,512]{1,0:T(8,128)S(1)}, f32[12,512,512]{1,2,0:T(8,128)}) fusion(f32[12,512,512]{1,2,0:T(8,128)} %get-tuple-element.310, f32[12,512]{1,0:T(8,128)S(1)} %get-tuple-element.309, bf16[512,12,64]{0,2,1:T(8,128)(2,1)} %bitcast.547, bf16[512,12,64]{0,2,1:T(8,128)(2,1)} %bitcast.544), kind=kOutput, calls=%fused_computation.7 | convolution fusion | flops 412084224 | bytes 26787840 | tf_op jit(solution)/shard_map/while/body/eval_jaxpr/qhd,khd->hqk/dot_general | solution.py:84
  361.6 6.4 reduce.30
  369.3 4.6 all-to-all-start.13
  374.0 9.6 %multiply_convert_fusion.1 = bf16[12,512,512]{1,2,0:T(8,128)(2,1)S(1)} fusion(f32[12,512,512]{1,2,0:T(8,128)} %get-tuple-element.317, f32[12,512]{1,0:T(8,128)S(1)} %get-tuple-element.316, f32[12,512,512]{1,2,0:T(8,128)} %get-tuple-element.310, f32[12,512]{1,0:T(8,128)S(1)} %get-tuple-element.309), kind=kLoop, calls=%fused_computation.6 | loop fusion | flops 12582912 | bytes 31506432 | tf_op jit(solution)/shard_map/while/body/eval_jaxpr/convert_element_type | solution.py:88
  383.6 3.7 multiply_convert_fusion.5
  388.6 6.3 reduce.32
  397.2 4.5 all-to-all-start.11
  405.2 3.9 multiply_convert_fusion.6
  411.5 7.5 reduce.31
  421.3 4.4 all-to-all-start.10
  452.4 12.3 %all-reduce.3 = (f32[2048]{0:T(1024)S(1)}, f32[2048]{0:T(1024)S(1)}) all-reduce(f32[2048]{0:T(1024)S(1)} %get-tuple-element.221, f32[2048]{0:T(1024)S(1)} %get-tuple-element.228), channel_id=1, replica_groups=mesh['dp'=8,'grp'=4] {'grp'}, use_global_device_ids=true, to_apply=%region_26.27 | all-reduce | flops 4096 | bytes 32768 | tf_op jit(solution)/shard_map/psum | solution.py:260
  466.6 5.8 convert_reduce_fusion.1
  481.6 3.6 collective-permute-done.4
  493.8 6.7 fusion.64
  500.5 8.9 %multiply_reduce_fusion = (f32[12,512]{1,0:T(8,128)S(1)}, f32[12,512,512]{1,2,0:T(8,128)}) fusion(f32[12,512,512]{1,2,0:T(8,128)} %get-tuple-element.303, f32[12,512]{1,0:T(8,128)S(1)} %copy-done.82, bf16[512,12,64]{0,2,1:T(8,128)(2,1)S(1)} %bitcast.549, bf16[512,12,64]{0,2,1:T(8,128)(2,1)S(1)} %bitcast.542), kind=kOutput, calls=%fused_computation.5 | convolution fusion | flops 412084224 | bytes 26787840 | tf_op jit(solution)/shard_map/while/body/eval_jaxpr/qhd,khd->hqk/dot_general | solution.py:84
  510.7 5.4 reduce.37
  517.5 4.4 all-to-all-start.16
  521.8 9.6 %multiply_convert_fusion = bf16[12,512,512]{1,2,0:T(8,128)(2,1)S(1)} fusion(f32[12,512,512]{1,2,0:T(8,128)} %get-tuple-element.320, f32[12,512]{1,0:T(8,128)S(1)} %get-tuple-element.319, f32[12,512,512]{1,2,0:T(8,128)} %get-tuple-element.303, f32[12,512]{1,0:T(8,128)S(1)} %copy-done.82), kind=kLoop, calls=%fused_computation.4 | loop fusion | flops 12582912 | bytes 31506432 | tf_op jit(solution)/shard_map/while/body/eval_jaxpr/convert_element_type | solution.py:88
  531.5 3.7 multiply_convert_fusion.2
  536.4 5.4 reduce.36
  546.8 4.2 all-to-all-start.15
  551.2 4.2 pad_maximum_fusion
  556.5 3.9 multiply_convert_fusion.3
  562.8 7.5 reduce.35
  572.6 4.2 all-to-all-start.14
  602.5 3.5 copy.216
  606.0 6.3 reduce.34
  614.7 4.2 all-to-all-start.17
  619.1 47.4 %all-reduce = (f32[2,768]{1,0:T(2,128)}, f32[2,768]{1,0:T(2,128)}, f32[2,768]{1,0:T(2,128)}) all-reduce(f32[2,768]{1,0:T(2,128)S(1)} %pad_maximum_fusion.4, f32[2,768]{1,0:T(2,128)S(1)} %pad_maximum_fusion.5, f32[2,768]{1,0:T(2,128)S(1)} %pad_maximum_fusion.6), channel_id=1, replica_groups=mesh['dp'=8,'grp'=4] {'dp','grp'}, use_global_device_ids=true, to_apply=%region_39.40 | all-reduce | flops 4608 | bytes 36864 | tf_op jit(solution)/shard_map/psum | solution.py:405
  673.6 37.8 %all-reduce.1 = (f32[2,2,192]{2,1,0:T(2,128)}, f32[2,768]{1,0:T(2,128)}, f32[2,192]{1,0:T(2,128)}, f32[2,192]{1,0:T(2,128)}, f32[2,192]{1,0:T(2,128)}) all-reduce(f32[2,2,192]{2,1,0:T(2,128)S(1)} %pad_maximum_fusion.8, f32[2,768]{1,0:T(2,128)S(1)} %pad_maximum_fusion.7, ...), channel_id=1, replica_groups=mesh['dp'=8,'grp'=4] {'dp'}, use_global_device_ids=true, to_apply=%region_35.36 | all-reduce | flops 3456 | bytes 27648 | tf_op jit(solution)/shard_map/psum | solution.py:392
  711.4 134.1 %all-reduce.12.cloned.1.call-done = (f32[2,1,192,576]{3,2,1,0:T(8,128)}, f32[2,1,192,768]{3,2,1,0:T(8,128)}, f32[2,1,768,192]{2,3,1,0:T(8,128)}) async-done(((f32[2,1,192,576]{3,2,1,0:T(8,128)}, f32[2,1,192,768]{3,2,1,0:T(8,128)}, f32[2,1,768,192]{2,3,1,0:T(8,128)}), (f32[2,1,192,576]{3,2,1,0:T(8,128)}, f32[2,1,192,768]{3,2,1,0:T(8,128)}, f32[2,1,768,192]{2,3,1,0:T(8,128)})) %all-reduce.12.cloned.1.call-update) | async-done | bytes 3244048 | tf_op jit(solution)/shard_map/psum | solution.py:392
  847.7 4.9 copy.320
  (452 shorter events, 220.6 us)
Async XLA Ops:
  7.2 16.0 %all-to-all-start = ((bf16[4,512,192]{1,2,0:T(8,128)(2,1)}), bf16[4,512,192]{1,2,0:T(8,128)(2,1)S(1)}, u32[]{:S(2)}, u32[]{:S(2)}) async-start(bf16[4,512,192]{1,2,0:T(8,128)(2,1)} %param.15), calls=%async_computation | async-start | bytes 1572864 | tf_op jit(solution)/shard_map/all_to_all | solution.py:160
  15.9 10.8 %copy-start.98 = (f32[2,2,192]{2,1,0:T(2,128)S(1)}, f32[2,2,192]{2,1,0:T(2,128)}, u32[]{:S(2)}) copy-start(f32[2,2,192]{2,1,0:T(2,128)} %param.19) | copy-start | bytes 9220
  23.2 15.1 %all-to-all-start.3 = ((bf16[4,512,192]{1,2,0:T(8,128)(2,1)}), bf16[4,512,192]{1,2,0:T(8,128)(2,1)S(1)}, u32[]{:S(2)}, u32[]{:S(2)}) async-start(bf16[4,512,192]{1,2,0:T(8,128)(2,1)} %bitcast.439), calls=%async_computation.3 | async-start | bytes 1572864 | tf_op jit(solution)/shard_map/all_to_all | solution.py:158
  28.9 14.3 %copy-start.89 = (f32[2,768]{1,0:T(2,128)S(1)}, f32[2,768]{1,0:T(2,128)}, u32[]{:S(2)}) copy-start(f32[2,768]{1,0:T(2,128)} %param.21) | copy-start | bytes 18436
  28.9 14.3 %copy-start.90 = (f32[2,768]{1,0:T(2,128)S(1)}, f32[2,768]{1,0:T(2,128)}, u32[]{:S(2)}) copy-start(f32[2,768]{1,0:T(2,128)} %param.23) | copy-start | bytes 18436
  28.9 14.3 %copy-start.91 = (f32[2,768]{1,0:T(2,128)S(1)}, f32[2,768]{1,0:T(2,128)}, u32[]{:S(2)}) copy-start(f32[2,768]{1,0:T(2,128)} %param.22) | copy-start | bytes 18436
  38.3 19.4 %copy-start.30 = (bf16[4,512,192]{1,2,0:T(8,128)(2,1)}, bf16[4,512,192]{1,2,0:T(8,128)(2,1)S(1)}, u32[]{:S(2)}) copy-start(bf16[4,512,192]{1,2,0:T(8,128)(2,1)S(1)} %all-to-all-done.3) | copy-start | bytes 2359300
  38.3 15.9 %all-to-all-start.2 = ((bf16[4,512,192]{1,2,0:T(8,128)(2,1)}), bf16[4,512,192]{1,2,0:T(8,128)(2,1)}, u32[]{:S(2)}, u32[]{:S(2)}) async-start(bf16[4,512,192]{1,2,0:T(8,128)(2,1)} %bitcast.440), calls=%async_computation.2 | async-start | bytes 1572864 | tf_op jit(solution)/shard_map/all_to_all | solution.py:157
  43.3 177.3 %copy-start.75 = (f32[768]{0:T(1024)}, f32[768]{0:T(1024)S(1)}, u32[]{:S(2)}) copy-start(f32[768]{0:T(1024)S(1)} %get-tuple-element.325) | copy-start | bytes 9220
  54.2 15.1 %all-to-all-start.1 = ((bf16[4,512,192]{1,2,0:T(8,128)(2,1)}), bf16[4,512,192]{1,2,0:T(8,128)(2,1)S(1)}, u32[]{:S(2)}, u32[]{:S(2)}) async-start(bf16[4,512,192]{1,2,0:T(8,128)(2,1)} %bitcast.441), calls=%async_computation.1 | async-start | bytes 1572864 | tf_op jit(solution)/shard_map/all_to_all | solution.py:159
  68.3 7.2 copy-start.81
  76.8 8.6 %copy-start.79 = (f32[512]{0:T(512)}, f32[512]{0:T(512)S(1)}, u32[]{:S(2)}) copy-start(f32[512]{0:T(512)S(1)} %add_rsqrt_fusion.3) | copy-start | bytes 6148
  79.4 10.9 %copy-start.101 = (f32[2,192]{1,0:T(2,128)S(1)}, f32[2,192]{1,0:T(2,128)}, u32[]{:S(2)}) copy-start(f32[2,192]{1,0:T(2,128)} %param.27) | copy-start | bytes 4612
  79.5 11.5 %copy-start.92 = (f32[2,768]{1,0:T(2,128)S(1)}, f32[2,768]{1,0:T(2,128)}, u32[]{:S(2)}) copy-start(f32[2,768]{1,0:T(2,128)} %param.25) | copy-start | bytes 18436
  79.5 11.5 %copy-start.102 = (f32[2,192]{1,0:T(2,128)S(1)}, f32[2,192]{1,0:T(2,128)}, u32[]{:S(2)}) copy-start(f32[2,192]{1,0:T(2,128)} %param.28) | copy-start | bytes 4612
  79.5 11.5 %copy-start.103 = (f32[2,192]{1,0:T(2,128)S(1)}, f32[2,192]{1,0:T(2,128)}, u32[]{:S(2)}) copy-start(f32[2,192]{1,0:T(2,128)} %param.29) | copy-start | bytes 4612
  86.8 15.1 %all-to-all-start.4 = ((bf16[4,2,49152]{2,1,0:T(2,128)(2,1)}), bf16[4,2,49152]{2,1,0:T(2,128)(2,1)S(1)}, u32[]{:S(2)}, u32[]{:S(2)}) async-start(bf16[4,2,49152]{2,1,0:T(2,128)(2,1)} %reshape.523), calls=%async_computation.4 | async-start | bytes 1572864 | tf_op jit(solution)/shard_map/all_to_all | solution.py:180
  91.0 12.8 %copy-start.95 = (f32[768]{0:T(1024)}, f32[768]{0:T(1024)S(1)}, u32[]{:S(2)}) copy-start(f32[768]{0:T(1024)S(1)} %get-tuple-element.241) | copy-start | bytes 9220
  91.0 40.5 %copy-start.83 = (f32[1,192]{1,0:T(1,128)}, f32[1,192]{1,0:T(1,128)S(1)}, u32[]{:S(2)}) copy-start(f32[1,192]{1,0:T(1,128)S(1)} %get-tuple-element.297) | copy-start | bytes 2308
  103.7 15.9 %copy-start.47 = (bf16[24,8,4,512]{3,1,2,0:T(8,128)(2,1)}, bf16[24,8,4,512]{3,1,2,0:T(8,128)(2,1)S(1)}, u32[]{:S(2)}) copy-start(bf16[24,8,4,512]{3,1,2,0:T(8,128)(2,1)S(1)} %copy.258) | copy-start | bytes 2359300
  103.8 15.9 %copy-start.109 = (bf16[2,1,768,192]{2,3,1,0:T(8,128)(2,1)S(1)}, bf16[2,1,768,192]{2,3,1,0:T(8,128)(2,1)}, u32[]{:S(2)}) copy-start(bf16[2,1,768,192]{2,3,1,0:T(8,128)(2,1)} %param.26) | copy-start | bytes 1769476
  121.4 17.4 %copy-start.14 = (f32[2048,192]{0,1:T(8,128)}, f32[2048,192]{0,1:T(8,128)S(1)}, u32[]{:S(2)}) copy-start(f32[2048,192]{0,1:T(8,128)S(1)} %get-tuple-element.308) | copy-start | bytes 4718596
  133.5 15.1 %all-to-all-start.5 = ((bf16[4,512,192]{1,2,0:T(8,128)(2,1)}), bf16[4,512,192]{1,2,0:T(8,128)(2,1)S(1)}, u32[]{:S(2)}, u32[]{:S(2)}) async-start(bf16[4,512,192]{1,2,0:T(8,128)(2,1)} %bitcast.438), calls=%async_computation.5 | async-start | bytes 1572864 | tf_op jit(solution)/shard_map/all_to_all | solution.py:160
  148.6 15.3 %all-to-all-start.8 = ((bf16[4,512,192]{1,2,0:T(8,128)(2,1)}), bf16[4,512,192]{1,2,0:T(8,128)(2,1)S(1)}, u32[]{:S(2)}, u32[]{:S(2)}) async-start(bf16[4,512,192]{1,2,0:T(8,128)(2,1)} %bitcast.435), calls=%async_computation.8 | async-start | bytes 1572864 | tf_op jit(solution)/shard_map/all_to_all | solution.py:158
  164.0 19.4 %copy-start.32 = (bf16[4,512,192]{1,2,0:T(8,128)(2,1)}, bf16[4,512,192]{1,2,0:T(8,128)(2,1)S(1)}, u32[]{:S(2)}) copy-start(bf16[4,512,192]{1,2,0:T(8,128)(2,1)S(1)} %all-to-all-done.8) | copy-start | bytes 2359300
  164.0 15.9 %all-to-all-start.7 = ((bf16[4,512,192]{1,2,0:T(8,128)(2,1)}), bf16[4,512,192]{1,2,0:T(8,128)(2,1)}, u32[]{:S(2)}, u32[]{:S(2)}) async-start(bf16[4,512,192]{1,2,0:T(8,128)(2,1)} %bitcast.436), calls=%async_computation.7 | async-start | bytes 1572864 | tf_op jit(solution)/shard_map/all_to_all | solution.py:157
  179.9 15.1 %all-to-all-start.6 = ((bf16[4,512,192]{1,2,0:T(8,128)(2,1)}), bf16[4,512,192]{1,2,0:T(8,128)(2,1)S(1)}, u32[]{:S(2)}, u32[]{:S(2)}) async-start(bf16[4,512,192]{1,2,0:T(8,128)(2,1)} %bitcast.437), calls=%async_computation.6 | async-start | bytes 1572864 | tf_op jit(solution)/shard_map/all_to_all | solution.py:159
  213.9 7.4 copy-start.41
  216.3 15.9 %all-to-all-start.9 = ((bf16[4,2,49152]{2,1,0:T(2,128)(2,1)}), bf16[4,2,49152]{2,1,0:T(2,128)(2,1)}, u32[]{:S(2)}, u32[]{:S(2)}) async-start(bf16[4,2,49152]{2,1,0:T(2,128)(2,1)} %reshape.525), calls=%async_computation.9 | async-start | bytes 1572864 | tf_op jit(solution)/shard_map/all_to_all | solution.py:180
  222.6 44.4 %copy-start.12 = (f32[4,24,8,512]{3,2,0,1:T(8,128)}, f32[4,24,8,512]{3,2,0,1:T(8,128)S(1)}, u32[]{:S(2)}) copy-start(f32[4,24,8,512]{3,2,0,1:T(8,128)S(1)} %copy.257) | copy-start | bytes 4718596
  238.4 15.9 %copy-start.48 = (bf16[24,8,4,512]{3,1,2,0:T(8,128)(2,1)}, bf16[24,8,4,512]{3,1,2,0:T(8,128)(2,1)S(1)}, u32[]{:S(2)}) copy-start(bf16[24,8,4,512]{3,1,2,0:T(8,128)(2,1)S(1)} %copy.259) | copy-start | bytes 2359300
  238.5 15.9 %copy-start.104 = (f32[1,192]{1,0:T(1,128)S(1)}, f32[1,192]{1,0:T(1,128)}, u32[]{:S(2)}) copy-start(f32[1,192]{1,0:T(1,128)} %get-tuple-element.300) | copy-start | bytes 2308
  238.5 15.9 %copy-start.110 = (bf16[2,1,768,192]{2,3,1,0:T(8,128)(2,1)S(1)}, bf16[2,1,768,192]{2,3,1,0:T(8,128)(2,1)}, u32[]{:S(2)}) copy-start(bf16[2,1,768,192]{2,3,1,0:T(8,128)(2,1)} %param.26) | copy-start | bytes 1769476
  256.7 22.9 %copy-start.100 = (f32[1,192]{1,0:T(1,128)S(1)}, f32[1,192]{1,0:T(1,128)}, u32[]{:S(2)}) copy-start(f32[1,192]{1,0:T(1,128)} %get-tuple-element.298) | copy-start | bytes 2308
  283.7 8.0 copy-start.69
  300.8 7.6 collective-permute-start.1
  302.0 7.4 collective-permute-start.2
  302.0 7.4 collective-permute-start
  326.6 6.9 copy-start.63
  343.6 25.8 %all-to-all-start.12 = ((bf16[4,2,49152]{2,1,0:T(2,128)(2,1)}), bf16[4,2,49152]{2,1,0:T(2,128)(2,1)S(1)}, u32[]{:S(2)}, u32[]{:S(2)}) async-start(bf16[4,2,49152]{2,1,0:T(2,128)(2,1)} %reshape.533), calls=%async_computation.12 | async-start | bytes 1572864 | tf_op jit(solution)/shard_map/all_to_all | solution.py:302
  347.1 11.6 %copy-start.26 = (bf16[512,768]{1,0:T(8,128)(2,1)S(1)}, bf16[512,768]{1,0:T(8,128)(2,1)}, u32[]{:S(2)}) copy-start(bf16[512,768]{1,0:T(8,128)(2,1)} %copy-done.25) | copy-start | bytes 2359300
  369.3 14.3 %copy-start.42 = (bf16[4,2,49152]{2,1,0:T(2,128)(2,1)}, bf16[4,2,49152]{2,1,0:T(2,128)(2,1)S(1)}, u32[]{:S(2)}) copy-start(bf16[4,2,49152]{2,1,0:T(2,128)(2,1)S(1)} %all-to-all-done.12) | copy-start | bytes 2359300
  369.3 27.9 %all-to-all-start.13 = ((bf16[4,2,49152]{2,1,0:T(2,128)(2,1)}), bf16[4,2,49152]{2,1,0:T(2,128)(2,1)}, u32[]{:S(2)}, u32[]{:S(2)}) async-start(bf16[4,2,49152]{2,1,0:T(2,128)(2,1)} %reshape.527), calls=%async_computation.13 | async-start | bytes 1572864 | tf_op jit(solution)/shard_map/all_to_all | solution.py:303
  397.2 8.0 copy-start.33
  397.2 24.1 %all-to-all-start.11 = ((bf16[4,2,49152]{2,1,0:T(2,128)(2,1)}), bf16[4,2,49152]{2,1,0:T(2,128)(2,1)}, u32[]{:S(2)}, u32[]{:S(2)}) async-start(bf16[4,2,49152]{2,1,0:T(2,128)(2,1)} %reshape.531), calls=%async_computation.11 | async-start | bytes 1572864 | tf_op jit(solution)/shard_map/all_to_all | solution.py:301
  411.5 14.2 %copy-start.9 = (bf16[2048,768]{1,0:T(8,128)(2,1)S(1)}, bf16[2048,768]{1,0:T(8,128)(2,1)}, u32[]{:S(2)}) copy-start(bf16[2048,768]{1,0:T(8,128)(2,1)} %copy-done.8) | copy-start | bytes 9437188
  421.3 23.0 %all-to-all-start.10 = ((bf16[4,2,49152]{2,1,0:T(2,128)(2,1)}), bf16[4,2,49152]{2,1,0:T(2,128)(2,1)}, u32[]{:S(2)}, u32[]{:S(2)}) async-start(bf16[4,2,49152]{2,1,0:T(2,128)(2,1)} %reshape.529), calls=%async_computation.10 | async-start | bytes 1572864 | tf_op jit(solution)/shard_map/all_to_all | solution.py:300
  452.4 14.3 %copy-start.96 = (f32[768]{0:T(1024)S(1)}, f32[768]{0:T(1024)}, u32[]{:S(2)}) copy-start(f32[768]{0:T(1024)} %copy-done.95) | copy-start | bytes 9220
  466.6 7.5 copy-start.70
  477.7 7.5 collective-permute-start.4
  478.8 7.4 collective-permute-start.5
  478.8 7.4 collective-permute-start.3
  481.6 6.7 copy-start.87
  517.5 29.3 %all-to-all-start.16 = ((bf16[4,2,49152]{2,1,0:T(2,128)(2,1)}), bf16[4,2,49152]{2,1,0:T(2,128)(2,1)}, u32[]{:S(2)}, u32[]{:S(2)}) async-start(bf16[4,2,49152]{2,1,0:T(2,128)(2,1)} %reshape.541), calls=%async_computation.16 | async-start | bytes 1572864 | tf_op jit(solution)/shard_map/all_to_all | solution.py:302
  535.2 8.0 copy-start.24
  543.2 8.0 copy-start.18
  546.8 25.9 %all-to-all-start.15 = ((bf16[4,2,49152]{2,1,0:T(2,128)(2,1)}), bf16[4,2,49152]{2,1,0:T(2,128)(2,1)}, u32[]{:S(2)}, u32[]{:S(2)}) async-start(bf16[4,2,49152]{2,1,0:T(2,128)(2,1)} %reshape.539), calls=%async_computation.15 | async-start | bytes 1572864 | tf_op jit(solution)/shard_map/all_to_all | solution.py:301
  551.0 160.4 %all-reduce.10.cloned.1.call-start = ((), (), s32[]{:S(2)}) async-start(), calls=%async_computation.18 | async-start | bytes 9437184 | tf_op jit(solution)/shard_map/psum | solution.py:405
  562.8 14.1 %copy-start.7 = (bf16[2048,768]{1,0:T(8,128)(2,1)S(1)}, bf16[2048,768]{1,0:T(8,128)(2,1)}, u32[]{:S(2)}) copy-start(bf16[2048,768]{1,0:T(8,128)(2,1)} %copy-done.6) | copy-start | bytes 9437188
  572.6 19.9 %all-to-all-start.14 = ((bf16[4,2,49152]{2,1,0:T(2,128)(2,1)}), bf16[4,2,49152]{2,1,0:T(2,128)(2,1)}, u32[]{:S(2)}, u32[]{:S(2)}) async-start(bf16[4,2,49152]{2,1,0:T(2,128)(2,1)} %reshape.537), calls=%async_computation.14 | async-start | bytes 1572864 | tf_op jit(solution)/shard_map/all_to_all | solution.py:300
  576.8 268.6 %all-reduce.12.cloned.1.call-start = ((), (), s32[]{:S(2)}) async-start(), calls=%async_computation.19 | async-start | bytes 6684672 | tf_op jit(solution)/shard_map/psum | solution.py:392
  606.0 12.9 %copy-start.93 = (f32[192]{0:T(256)S(1)}, f32[192]{0:T(256)}, u32[]{:S(2)}) copy-start(f32[192]{0:T(256)} %get-tuple-element.234) | copy-start | bytes 2308
  606.0 12.9 %copy-start.99 = (f32[192]{0:T(256)S(1)}, f32[192]{0:T(256)}, u32[]{:S(2)}) copy-start(f32[192]{0:T(256)} %get-tuple-element.273) | copy-start | bytes 2308
  614.7 51.8 %all-to-all-start.17 = ((bf16[4,2,49152]{2,1,0:T(2,128)(2,1)}), bf16[4,2,49152]{2,1,0:T(2,128)(2,1)}, u32[]{:S(2)}, u32[]{:S(2)}) async-start(bf16[4,2,49152]{2,1,0:T(2,128)(2,1)} %reshape.535), calls=%async_computation.17 | async-start | bytes 1572864 | tf_op jit(solution)/shard_map/all_to_all | solution.py:303
  (74 other events, 205.8 us)
Sparse Core Ops, SparseCore 0:
  558.0 147.8 all-reduce.9
  711.5 133.8 all-reduce.11
